TPU v7x, 128 devices: a whole 4x4x4 slice. The times are simulated.
128 devices in a mesh: freq: 4 (over z_hi, core), pos: 32 (over x, y, z_lo).
Axes of the slice: x: 4, y: 4, z: 4 (z_hi: 2, z_lo: 2; z = z_hi * 2 + z_lo), core: 2. Of those that a mesh axis runs over, the one named last changes fastest.
Arguments:
- spectra: bfloat16 [16, 2, 256, 32768], P(None, None, 'freq', 'pos'), may hold values from -6 to 6
- green: bfloat16 [16, 32768, 2048], P('freq', 'pos'), may hold values from -0.0234375 to 0.0234375
- recorded: bfloat16 [256, 1024, 512], P('pos', 'freq'), may hold values from -6 to 6
- filter_taps: float32 [256, 11], P('pos'), may hold values from -3 to 3
Outputs:
- primaries: bfloat16 [256, 1024, 512], P('pos', 'freq')
All inputs are finite; a program needn't handle non-finite values.
Results may differ from a plain program's by a relative error of at most 0.001.
Values may be sent and summed in bfloat16 or wider, within the bound.
No kernel may reach another device: no remote copies, remote signals or barrier semaphores. Data moves between devices by JAX's collectives and lax.ppermute only.
A program may use at most 128 MiB of HBM per device.

v0:
```python
import jax
import jax.numpy as jnp
from jax import lax
from jax.sharding import Mesh
from jax.sharding import PartitionSpec as P

BAND_START = 32
FREQ = ("freq_0", "freq_1")
POS = ("pos_0", "pos_1", "pos_2")


def sum_by_axis(subtotal, axes):
    for axis in axes:
        subtotal = lax.psum_scatter(subtotal, axis, scatter_dimension=0, tiled=True)
    return subtotal


def cut_along(array, dim, devices):
    before, after = (array.shape[:dim], array.shape[dim + 1 :])
    return jnp.moveaxis(array.reshape(*before, devices, -1, *after), dim, 0)


def joined_along(parts, dim):
    shape = list(parts.shape[1:])
    shape[dim] *= parts.shape[0]
    return jnp.moveaxis(parts, 0, dim).reshape(shape)


def moved_by_axis(parts, axes, order):
    shape = [lax.axis_size(a) for a in axes]
    parts = parts.reshape(*shape, *parts.shape[1:])
    for k in order:
        parts = lax.all_to_all(parts, axes[k], split_axis=k, concat_axis=k, tiled=True)
    return parts.reshape(-1, *parts.shape[len(axes) :])


def core_and_chips(array, groups, order, split_dim, concat_dim):
    devices = lax.axis_size(groups[0]) * lax.axis_size(groups[1])
    parts = cut_along(array, split_dim, devices)
    return joined_along(moved_by_axis(parts, groups, order), concat_dim)


def phase_table(first_freq, freq_count, total_freqs, samples):
    bins = BAND_START + first_freq + jnp.arange(freq_count, dtype=jnp.int32)
    sample_index = jnp.arange(samples, dtype=jnp.int32)
    phase = bins[:, None] * sample_index[None, :] % samples
    angle = 2.0 * jnp.pi / samples * phase.astype(jnp.float32)
    scale = 1.0 / jnp.sqrt(jnp.float32(total_freqs))
    return jnp.stack([jnp.cos(angle), -jnp.sin(angle)], 1) * scale


def on_device(spectra, green, recorded, filter_taps):
    regrouped = lax.all_to_all(spectra, FREQ, split_axis=0, concat_axis=2, tiled=True)
    half_cols = green.shape[2] // 2
    product = jnp.einsum("fisk,fkr->sfir", regrouped, green, preferred_element_type=jnp.float32)
    real_part = product[:, :, 0, :half_cols] - product[:, :, 1, half_cols:]
    imag_part = product[:, :, 0, half_cols:] + product[:, :, 1, :half_cols]
    own_share = sum_by_axis(jnp.stack([real_part, imag_part], 2), POS)
    samples = recorded.shape[2]
    total_freqs = spectra.shape[0]
    spread = core_and_chips(own_share, ("freq_0", "freq_1"), (1, 0), 3, 1)
    table = phase_table(0, total_freqs, total_freqs, samples)
    traces = jnp.einsum("sfir,fit->srt", spread, table, precision=lax.Precision.HIGHEST)
    tap_count = filter_taps.shape[1]
    margin = (tap_count - 1) // 2
    padded = jnp.pad(traces, ((0, 0), (0, 0), (margin, margin)))
    result = recorded.astype(jnp.float32)
    for lag in range(tap_count):
        result = result - filter_taps[:, lag][:, None, None] * padded[:, :, lag : lag + samples]
    return result.astype(jnp.bfloat16)


def solution(mesh):
    torus = Mesh(
        mesh.devices.reshape(2, 2, 4, 4, 2), ("freq_0", "freq_1", "pos_0", "pos_1", "pos_2")
    )
    placed = (P(None, None, FREQ, POS), P(FREQ, POS, None), P(POS, FREQ, None), P(POS, None))
    return jax.shard_map(
        on_device, mesh=torus, in_specs=placed, out_specs=P(POS, FREQ, None), check_vma=False
    )
```

profile of v0, /device:TPU:0, one launch (start us, length us, event | category | flops | bytes accessed | tf_op | source)
XLA Modules:
  0.0 406.5 jit_solution(1218572337466034315)
XLA Ops:
  6.5 54.9 %all_to_all.28 = bf16[16,2,64,1024]{3,2,1,0:T(8,128)(2,1)S(1)} all-to-all(bf16[16,2,64,1024]{3,2,1,0:T(8,128)(2,1)} %param.4), channel_id=1, replica_groups=mesh['freq_0'=2,'freq_1'=2,'pos_0'=4,'pos_1'=4,'pos_2'=2] {'freq_0','fre..., dimensions={0} | all-to-all | bytes 8388608 | tf_op jit(solution)/shard_map/all_to_all | solution.py:53
  61.4 2.4 copy.19
  63.8 18.0 %fusion.2 = f32[256,4,2,2048]{0,3,2,1:T(8,128)} fusion(bf16[4,2,256,1024]{3,2,1,0:T(8,128)(2,1)} %bitcast.36, bf16[4,1024,2048]{2,1,0:T(8,128)(2,1)} %param.5), kind=kOutput, calls=%fused_computation.13 | convolution fusion | flops 8589934592 | bytes 37748736 | tf_op jit(solution)/shard_map/fisk,fkr->sfir/dot_general | solution.py:55
  81.8 9.2 %slice_subtract_fusion = (f32[256,4,1,1024]{0,3,2,1:T(8,128)S(1)}, f32[256,4,1,1024]{0,3,2,1:T(8,128)}) fusion(f32[256,4,2,2048]{0,3,2,1:T(8,128)} %fusion.2), kind=kLoop, calls=%fused_computation.36 | loop fusion | flops 2097152 | bytes 25165824 | tf_op jit(solution)/shard_map/sub | solution.py:56
  91.0 6.1 %pad_maximum_fusion = f32[256,4,2,1024]{0,3,2,1:T(8,128)} fusion(f32[256,4,1,1024]{0,3,2,1:T(8,128)} %get-tuple-element.17, f32[256,4,1,1024]{0,3,2,1:T(8,128)S(1)} %get-tuple-element.16), kind=kLoop, calls=%fused_computation.2 | loop fusion | flops 2097152 | bytes 16777216 | tf_op jit(solution)/shard_map/stack | solution.py:58
  97.1 10.5 %copy.21 = f32[256,4,2,1024]{3,1,2,0:T(4,128)} copy(f32[256,4,2,1024]{0,3,2,1:T(8,128)} %pad_maximum_fusion) | data formatting | bytes 16777216 | tf_op jit(solution)/shard_map/stack | solution.py:58
  107.6 0.0 all-reduce.8.cloned.1.call-update
  107.7 0.0 all-reduce.10.cloned.1.call-start
  107.7 0.5 copy-done.4
  108.3 0.6 dynamic-slice
  109.5 157.7 %all-reduce.8.cloned.1.call-done = f32[256,4,2,1024]{3,1,2,0:T(4,128)} async-done(((f32[256,4,2,1024]{3,1,2,0:T(4,128)}), f32[256,4,2,1024]{3,1,2,0:T(4,128)}) %all-reduce.8.cloned.1.call-update) | async-done | bytes 8388624
  267.2 3.2 constant_dynamic-slice_fusion.2
  270.4 0.0 all-reduce.10.cloned.1.call-update
  270.5 0.0 all-reduce.12.cloned.1.call-start
  270.5 0.6 dynamic-slice.2
  271.7 57.4 %all-reduce.10.cloned.1.call-done = f32[64,4,2,1024]{3,1,2,0:T(4,128)} async-done(((f32[64,4,2,1024]{3,1,2,0:T(4,128)}), f32[64,4,2,1024]{3,1,2,0:T(4,128)}) %all-reduce.10.cloned.1.call-update) | async-done | bytes 2097168
  329.2 1.9 constant_dynamic-slice_fusion.1
  331.1 0.7 dynamic-slice.4
  332.5 34.4 %all-reduce.12.cloned.1.call-done = f32[16,4,2,1024]{3,1,2,0:T(4,128)} async-done(((f32[16,4,2,1024]{3,1,2,0:T(4,128)}), f32[16,4,2,1024]{3,1,2,0:T(4,128)}) %all-reduce.12.cloned.1.call-update) | async-done | bytes 524304
  366.8 1.0 constant_dynamic-slice_fusion
  367.8 0.2 reshape.130
  368.0 0.2 copy.23
  368.2 4.1 %all_to_all.29 = f32[2,2,8,4,2,256]{5,2,4,3,0,1:T(8,128)S(1)} all-to-all(f32[2,2,8,4,2,256]{5,2,4,3,0,1:T(8,128)S(1)} %copy.24), channel_id=1, replica_groups=mesh['freq_0'=2,'freq_1'=2,'pos_0'=4,'pos_1'=4,'pos_2'=2] {'freq_1'}, dimensions={1} | all-to-all | bytes 524288 | tf_op jit(solution)/shard_map/all_to_all | solution.py:33
  372.3 0.7 copy.25
  373.0 4.1 %all-to-all-start.2 = ((f32[2,2,8,4,2,256]{5,2,4,3,1,0:T(8,128)}), f32[2,2,8,4,2,256]{5,2,4,3,1,0:T(8,128)S(1)}, u32[]{:S(2)}, u32[]{:S(2)}) async-start(f32[2,2,8,4,2,256]{5,2,4,3,1,0:T(8,128)} %copy.25), calls=%async_computation.2 | async-start | bytes 524288 | tf_op jit(solution)/shard_map/all_to_all | solution.py:33
  377.1 0.2 fusion.38
  377.3 0.3 slice_reduce_fusion.10
  377.7 6.4 %all-to-all-done.2 = f32[2,2,8,4,2,256]{5,2,4,3,1,0:T(8,128)S(1)} async-done(((f32[2,2,8,4,2,256]{5,2,4,3,1,0:T(8,128)}), f32[2,2,8,4,2,256]{5,2,4,3,1,0:T(8,128)S(1)}, u32[]{:S(2)}, u32[]{:S(2)}) %all-to-all-start.2) | async-done | bytes 262176 | tf_op jit(solution)/shard_map/all_to_all | solution.py:33
  384.1 0.2 copy.34
  384.3 0.1 reshape.126
  384.4 3.5 convolution_bitcast_fusion
  387.9 12.1 %fusion.26 = bf16[8,256,512]{2,1,0:T(8,128)(2,1)} fusion(f32[8,256,512]{2,1,0:T(8,128)S(1)} %convolution_bitcast_fusion, bf16[8,256,512]{2,1,0:T(8,128)(2,1)S(1)} %copy-done, f32[8]{0:T(128)S(1)} %get-tuple-element.14, f32[8]{0:T(128)S(1)} %get-tuple-element.15, f32[8]{0:T(128)S(1)} %get-tuple-element.6, f32[8]{0:T(128)S(1)} %get-tuple-element.7, ...), kind=kLoop, calls=%fused_computation.37 | loop fusion | flops 25165824 | bytes 8388960 | tf_op jit(solution)/shard_map/convert_element_type | solution.py:70
  (13 shorter events, 0.1 us)
Async XLA Ops:
  6.5 260.7 %all-reduce.8.cloned.1.call-start = ((), (), s32[]{:S(2)}) async-start(), calls=%async_computation.3 | async-start | bytes 16777216
  107.6 0.7 copy-start.4
  107.6 162.9 %copy-start.3 = (u32[128]{0:T(128)S(1)}, u32[128]{0:T(128)}, u32[]{:S(2)}) copy-start(u32[128]{0:T(128)} %constant.34) | copy-start | bytes 1540
  107.6 223.4 %copy-start.2 = (u32[128]{0:T(128)S(1)}, u32[128]{0:T(128)}, u32[]{:S(2)}) copy-start(u32[128]{0:T(128)} %constant.38) | copy-start | bytes 1540
  107.7 221.5 %all-reduce.10.cloned.1.call-start = ((), (), s32[]{:S(2)}) async-start(), calls=%async_computation.4 | async-start | bytes 4194304
  270.4 106.9 %copy-start.1 = (f32[8,11]{1,0:T(8,128)S(1)}, f32[8,11]{1,0:T(8,128)}, u32[]{:S(2)}) copy-start(f32[8,11]{1,0:T(8,128)} %param.7) | copy-start | bytes 1060
  270.5 96.4 %all-reduce.12.cloned.1.call-start = ((), (), s32[]{:S(2)}) async-start(), calls=%async_computation.5 | async-start | bytes 1048576
  368.0 19.9 %copy-start = (bf16[8,256,512]{2,1,0:T(8,128)(2,1)S(1)}, bf16[8,256,512]{2,1,0:T(8,128)(2,1)}, u32[]{:S(2)}) copy-start(bf16[8,256,512]{2,1,0:T(8,128)(2,1)} %param.6) | copy-start | bytes 6291460
  373.0 11.1 %all-to-all-start.2 = ((f32[2,2,8,4,2,256]{5,2,4,3,1,0:T(8,128)}), f32[2,2,8,4,2,256]{5,2,4,3,1,0:T(8,128)S(1)}, u32[]{:S(2)}, u32[]{:S(2)}) async-start(f32[2,2,8,4,2,256]{5,2,4,3,1,0:T(8,128)} %copy.25), calls=%async_computation.2 | async-start | bytes 524288 | tf_op jit(solution)/shard_map/all_to_all | solution.py:33
Sparse Core Ops, SparseCore 0:
  107.8 159.4 all-reduce.7
  270.6 58.5 all-reduce.9
  331.6 35.1 all-reduce.11
where the time goes:
time: 407 us; the launch traced here: 406 us
  waiting for transfers between devices  256 us (63%)
  blocking collectives  59 us (14%)
  other arithmetic  27.6 us (7%)
  local copies, waits for them, and re-layouts  23 us (6%)
  matrix products  21.5 us (5%)
  between operations  15.2 us (4%)
  starting transfers between devices  4.21 us (1%)
    unnamed x6, waiting for transfers between devices  250 us
    all_to_all x1, blocking collectives, on_device(): lax.all_to_all(spectra, FREQ, split_axis=0, concat_axis=2, tiled=True)  54.9 us
    dot_general x1, matrix products, on_device(): jnp.einsum('fisk,fkr->sfir', regrouped, green, preferred_element_type=jnp...  18 us
    convert_element_type x1, other arithmetic, on_device(): return result.astype(jnp.bfloat16)  12.1 us
    another operation x1, local copies, waits for them, and re-layouts, on_device(): own_share = sum_by_axis(jnp.stack([real_part, imag_part], 2), POS)  10.5 us
    sub x1, other arithmetic, on_device(): real_part = product[:, :, 0, :half_cols] - product[:, :, 1, half_cols:]  9.15 us
    unnamed x16, local copies, waits for them, and re-layouts  8.49 us
  transfers between devices with their start and end apart: 4, of which 4 were waited for; matrix products, arithmetic and copies ran while one was open for 1% of the time, Pallas kernels for 0%

commit v1 on v0

--- a/solution.py
+++ b/solution.py
@@ -50,7 +50,10 @@
 
 
 def on_device(spectra, green, recorded, filter_taps):
-    regrouped = lax.all_to_all(spectra, FREQ, split_axis=0, concat_axis=2, tiled=True)
+    regrouped = jnp.concatenate(
+        lax.all_to_all(jnp.stack(jnp.split(spectra, lax.axis_size(FREQ), axis=0)), FREQ, 0, 0),
+        axis=2,
+    )
     half_cols = green.shape[2] // 2
     product = jnp.einsum("fisk,fkr->sfir", regrouped, green, preferred_element_type=jnp.float32)
     real_part = product[:, :, 0, :half_cols] - product[:, :, 1, half_cols:]

time: 407 us -> 268 us (0.66)
  waiting for transfers between devices: 256 us -> 138 us
  local copies, waits for them, and re-layouts: 23 us -> 5.37 us
    unnamed x6 -> x3, waiting for transfers between devices: 250 us -> 0.05 us
    reduce_scatter x0 -> x3, waiting for transfers between devices: none -> 131 us  [sum_by_axis(): subtotal = lax.psum_scatter(subtotal, axis, scatter_dimension=0, tiled=True)]
    unnamed x16 -> x4, local copies, waits for them, and re-layouts: 8.49 us -> 0.01 us
    another operation x1, local copies, waits for them, and re-layouts: 10.5 us -> 2.87 us  [on_device(): jnp.stack(jnp.split(spectra, lax.axis_size(FREQ), axis=0))]
  transfers between devices with their start and end apart: 4 -> 4, of which waited for: 4 -> 4; matrix products, arithmetic and copies ran while one was open for 1% -> 0% of each run, Pallas kernels for 0% -> 0%
where the time goes in v1:
time: 268 us
  waiting for transfers between devices  138 us (51%)
  blocking collectives  58.6 us (22%)
  other arithmetic  29.8 us (11%)
  matrix products  19.1 us (7%)
  between operations  13.2 us (5%)
  local copies, waits for them, and re-layouts  5.37 us (2%)
  starting transfers between devices  4.21 us (2%)
    reduce_scatter x3, waiting for transfers between devices, sum_by_axis(): subtotal = lax.psum_scatter(subtotal, axis, scatter_dimension=0, tiled=True)  131 us
    all_to_all x1, blocking collectives, on_device(): lax.all_to_all(jnp.stack(jnp.split(spectra, lax.axis_size(FREQ), axis=0))...  54.7 us
    dot_general x1, matrix products, on_device(): jnp.einsum('fisk,fkr->sfir', regrouped, green, preferred_element_type=jnp...  15.6 us
    convert_element_type x1, other arithmetic, on_device(): return result.astype(jnp.bfloat16)  12.1 us
    sub x1, other arithmetic, on_device(): real_part = product[:, :, 0, :half_cols] - product[:, :, 1, half_cols:]  10.3 us
    another operation x1, other arithmetic, on_device(): own_share = sum_by_axis(jnp.stack([real_part, imag_part], 2), POS)  6.65 us
    all_to_all x1, waiting for transfers between devices, moved_by_axis(): lax.all_to_all(parts, axes[k], split_axis=k, concat_axis=k, tiled=True)  6.42 us
  transfers between devices with their start and end apart: 4, of which 4 were waited for; matrix products, arithmetic and copies ran while one was open for 0% of the time, Pallas kernels for 0%

profile of v1, /device:TPU:0, one launch (start us, length us, event | category | flops | bytes accessed | tf_op | source)
XLA Modules:
  0.0 267.9 jit_solution(11939591765964721156)
XLA Ops:
  6.5 0.0 reduce-scatter.4.cloned.1.call-start
  6.5 2.9 %slice_bitcast_fusion.3 = (bf16[1,4,2,64,1024]{4,3,2,1,0:T(8,128)(2,1)S(1)}, bf16[1,4,2,64,1024]{4,3,2,1,0:T(8,128)(2,1)S(1)}, bf16[1,4,2,64,1024]{4,3,2,1,0:T(8,128)(2,1)S(1)}, bf16[1,4,2,64,1024]{4,3,2,1,0:T(8,128)(2,1)S(1)}) fusion(bf16[16,2,64,1024]{3,2,1,0:T(8,128)(2,1)} %param.4), kind=kLoop, calls=%fused_computation.43 | loop fusion | bytes 8388608 | tf_op jit(solution)/shard_map/stack | solution.py:54
  9.4 0.6 pad_maximum_fusion.1
  10.0 54.7 %all_to_all.15 = bf16[4,4,2,64,1024]{4,3,2,1,0:T(8,128)(2,1)S(1)} all-to-all(bf16[4,4,2,64,1024]{4,3,2,1,0:T(8,128)(2,1)S(1)} %pad_maximum_fusion.1), channel_id=1, replica_groups=mesh['freq_0'=2,'freq_1'=2,'pos_0'=4,'pos_1'=4,'pos_2'=2] {'freq_0','fre..., dimensions={0} | all-to-all | bytes 8388608 | tf_op jit(solution)/shard_map/all_to_all | solution.py:54
  64.7 0.4 copy.9
  65.1 15.6 %fusion.2 = f32[256,4,2,2048]{3,0,2,1:T(8,128)} fusion(bf16[4,2,256,1024]{3,2,1,0:T(8,128)(2,1)S(1)} %bitcast.37, bf16[4,1024,2048]{2,1,0:T(8,128)(2,1)} %param.5), kind=kOutput, calls=%fused_computation.13 | convolution fusion | flops 8589934592 | bytes 37748736 | tf_op jit(solution)/shard_map/fisk,fkr->sfir/dot_general | solution.py:58
  80.8 10.3 %slice_subtract_fusion = (f32[256,4,1,1024]{3,0,2,1:T(8,128)S(1)}, f32[256,4,1,1024]{3,0,2,1:T(8,128)}) fusion(f32[256,4,2,2048]{3,0,2,1:T(8,128)} %fusion.2), kind=kLoop, calls=%fused_computation.36 | loop fusion | flops 2097152 | bytes 25165824 | tf_op jit(solution)/shard_map/sub | solution.py:59
  91.1 6.7 %pad_maximum_fusion = f32[256,4,2,1024]{3,0,2,1:T(8,128)} fusion(f32[256,4,1,1024]{3,0,2,1:T(8,128)} %get-tuple-element.17, f32[256,4,1,1024]{3,0,2,1:T(8,128)S(1)} %get-tuple-element.16), kind=kLoop, calls=%fused_computation.2 | loop fusion | flops 2097152 | bytes 16777216 | tf_op jit(solution)/shard_map/stack | solution.py:61
  97.7 0.0 reduce-scatter.4.cloned.1.call-update
  97.7 0.0 copy-start.1
  97.8 0.0 reduce-scatter.6.cloned.1.call-start
  97.8 79.9 %reduce-scatter.4.cloned.1.call-done = f32[64,4,2,1024]{3,0,2,1:T(8,128)} async-done(((f32[256,4,2,1024]{3,0,2,1:T(8,128)}), f32[64,4,2,1024]{3,0,2,1:T(8,128)}) %reduce-scatter.4.cloned.1.call-update) | async-done | bytes 2097168 | tf_op jit(solution)/shard_map/reduce_scatter | solution.py:14
  177.8 0.0 reduce-scatter.6.cloned.1.call-update
  177.8 0.0 copy-start
  177.8 0.0 reduce-scatter.8.cloned.1.call-start
  177.8 31.8 %reduce-scatter.6.cloned.1.call-done = f32[16,4,2,1024]{3,0,2,1:T(8,128)} async-done(((f32[64,4,2,1024]{3,0,2,1:T(8,128)}), f32[16,4,2,1024]{3,0,2,1:T(8,128)}) %reduce-scatter.6.cloned.1.call-update) | async-done | bytes 524304 | tf_op jit(solution)/shard_map/reduce_scatter | solution.py:14
  209.7 0.0 reduce-scatter.8.cloned.1.call-update
  209.7 19.3 %reduce-scatter.8.cloned.1.call-done = f32[8,4,2,1024]{3,0,2,1:T(8,128)} async-done(((f32[16,4,2,1024]{3,0,2,1:T(8,128)}), f32[8,4,2,1024]{3,0,2,1:T(8,128)}) %reduce-scatter.8.cloned.1.call-update) | async-done | bytes 262160 | tf_op jit(solution)/shard_map/reduce_scatter | solution.py:14
  229.0 1.0 copy.11
  230.0 3.9 %all_to_all.16 = f32[2,2,8,4,2,256]{5,2,0,4,3,1:T(8,128)S(1)} all-to-all(f32[2,2,8,4,2,256]{5,2,0,4,3,1:T(8,128)S(1)} %copy.11), channel_id=1, replica_groups=mesh['freq_0'=2,'freq_1'=2,'pos_0'=4,'pos_1'=4,'pos_2'=2] {'freq_1'}, dimensions={1} | all-to-all | bytes 524288 | tf_op jit(solution)/shard_map/all_to_all | solution.py:33
  233.9 0.7 copy.12
  234.6 4.1 %all-to-all-start.2 = ((f32[2,2,8,4,2,256]{5,2,1,4,3,0:T(8,128)}), f32[2,2,8,4,2,256]{5,2,1,4,3,0:T(8,128)S(1)}, u32[]{:S(2)}, u32[]{:S(2)}) async-start(f32[2,2,8,4,2,256]{5,2,1,4,3,0:T(8,128)} %copy.12), calls=%async_computation.5 | async-start | bytes 524288 | tf_op jit(solution)/shard_map/all_to_all | solution.py:33
  238.8 0.2 fusion.39
  239.0 0.0 copy-done.1
  239.0 0.3 slice_reduce_fusion.10
  239.3 6.4 %all-to-all-done.2 = f32[2,2,8,4,2,256]{5,2,1,4,3,0:T(8,128)S(1)} async-done(((f32[2,2,8,4,2,256]{5,2,1,4,3,0:T(8,128)}), f32[2,2,8,4,2,256]{5,2,1,4,3,0:T(8,128)S(1)}, u32[]{:S(2)}, u32[]{:S(2)}) %all-to-all-start.2) | async-done | bytes 262176 | tf_op jit(solution)/shard_map/all_to_all | solution.py:33
  245.8 3.5 %convolution_bitcast_fusion = f32[8,256,512]{2,1,0:T(8,128)S(1)} fusion(f32[8,16,2,256]{3,0,2,1:T(8,128)S(1)} %bitcast.38, f32[16,1,512]{2,0,1:T(8,128)S(1)} %get-tuple-element.23, f32[16,1,512]{2,0,1:T(8,128)S(1)} %get-tuple-element.22), kind=kOutput, calls=%fused_computation.39 | convolution fusion | flops 402685952 | bytes 4521984 | tf_op jit(solution)/shard_map/sfir,fit->srt/dot_general | solution.py:66
  249.3 0.0 copy-done
  249.3 12.1 %fusion.26 = bf16[8,256,512]{2,1,0:T(8,128)(2,1)} fusion(f32[8,256,512]{2,1,0:T(8,128)S(1)} %convolution_bitcast_fusion, bf16[8,256,512]{2,1,0:T(8,128)(2,1)S(1)} %copy-done, f32[8]{0:T(128)S(1)} %get-tuple-element.14, f32[8]{0:T(128)S(1)} %get-tuple-element.15, f32[8]{0:T(128)S(1)} %get-tuple-element.6, f32[8]{0:T(128)S(1)} %get-tuple-element.7, ...), kind=kLoop, calls=%fused_computation.38 | loop fusion | flops 25165824 | bytes 8388960 | tf_op jit(solution)/shard_map/convert_element_type | solution.py:73
  (2 shorter events, 0.0 us)
Async XLA Ops:
  6.5 171.2 %reduce-scatter.4.cloned.1.call-start = ((), (), s32[]{:S(2)}) async-start(), calls=%async_computation.6 | async-start | bytes 10485760 | tf_op jit(solution)/shard_map/reduce_scatter | solution.py:14
  97.7 141.2 %copy-start.1 = (f32[8,11]{1,0:T(8,128)S(1)}, f32[8,11]{1,0:T(8,128)}, u32[]{:S(2)}) copy-start(f32[8,11]{1,0:T(8,128)} %param.7) | copy-start | bytes 1060
  97.8 111.9 %reduce-scatter.6.cloned.1.call-start = ((), (), s32[]{:S(2)}) async-start(), calls=%async_computation.7 | async-start | bytes 2621440 | tf_op jit(solution)/shard_map/reduce_scatter | solution.py:14
  177.8 71.5 %copy-start = (bf16[8,256,512]{2,1,0:T(8,128)(2,1)S(1)}, bf16[8,256,512]{2,1,0:T(8,128)(2,1)}, u32[]{:S(2)}) copy-start(bf16[8,256,512]{2,1,0:T(8,128)(2,1)} %param.6) | copy-start | bytes 6291460
  177.8 51.2 %reduce-scatter.8.cloned.1.call-start = ((), (), s32[]{:S(2)}) async-start(), calls=%async_computation.8 | async-start | bytes 786432 | tf_op jit(solution)/shard_map/reduce_scatter | solution.py:14
  234.6 11.1 %all-to-all-start.2 = ((f32[2,2,8,4,2,256]{5,2,1,4,3,0:T(8,128)}), f32[2,2,8,4,2,256]{5,2,1,4,3,0:T(8,128)S(1)}, u32[]{:S(2)}, u32[]{:S(2)}) async-start(f32[2,2,8,4,2,256]{5,2,1,4,3,0:T(8,128)} %copy.12), calls=%async_computation.5 | async-start | bytes 524288 | tf_op jit(solution)/shard_map/all_to_all | solution.py:33
Sparse Core Ops, SparseCore 0:
  97.9 79.8 reduce-scatter.3
  180.2 29.4 reduce-scatter.5
  212.0 16.9 reduce-scatter.7
